TPU v7x, 128 devices: a whole 4x4x4 slice. The times are simulated.
128 devices in a mesh: fsdp: 32 (over z_lo, x, y), dp: 4 (over z_hi, core).
Axes of the slice: x: 4, y: 4, z: 4 (z_hi: 2, z_lo: 2; z = z_hi * 2 + z_lo), core: 2. Of those that a mesh axis runs over, the one named last changes fastest.
Arguments:
- teacher_hidden: bfloat16 [1024, 8192], P(('fsdp', 'dp'))
- student_hidden: bfloat16 [1024, 4096], P(('fsdp', 'dp'))
- teacher_head: bfloat16 [8192, 65536], P('dp', 'fsdp'), may hold values from -0.1875 to 0.1875
- student_head: bfloat16 [4096, 65536], P('dp', 'fsdp'), may hold values from -0.25 to 0.25
- actions: int32 [1024], replicated, may hold values from 0 to 65535
- advantages: float32 [1024], replicated, may hold values from -0.21875 to 0.21875
- loss_mask: int32 [1024], replicated, may hold values 0 or 1
Outputs:
- token_loss: float32 [1024], P('dp')
- head_grad: float32 [4096, 65536], P('dp', 'fsdp')
- hidden_grad: bfloat16 [1024, 4096], P('fsdp', 'dp')
All inputs are finite; a program needn't handle non-finite values.
Results may differ from a plain program's by a relative error of at most 0.0048.
Values may be sent and summed in bfloat16 or wider, within the bound.
No kernel may reach another device: no remote copies, remote signals or barrier semaphores. Data moves between devices by JAX's collectives and lax.ppermute only.
A program may use at most 128 MiB of HBM per device.

v0:
```python
import jax
import jax.numpy as jnp
from jax import lax
from jax.sharding import PartitionSpec as P

kl_weight = 0.5


def shards(
    teacher_hidden, student_hidden, teacher_head, student_head, actions, advantages, loss_mask
):
    teacher_part, student_part = (
        lax.all_to_all(teacher_hidden, "dp", split_axis=1, concat_axis=0, tiled=True),
        lax.all_to_all(student_hidden, "dp", split_axis=1, concat_axis=0, tiled=True),
    )
    teacher_rows, student_rows = (
        lax.all_gather(teacher_part, "fsdp", axis=0, tiled=True),
        lax.all_gather(student_part, "fsdp", axis=0, tiled=True),
    )
    total_rows = teacher_rows.shape[0]
    share = total_rows // lax.axis_size("dp")
    teacher_partial = jnp.dot(teacher_rows, teacher_head, preferred_element_type=jnp.float32)
    student_partial = jnp.dot(student_rows, student_head, preferred_element_type=jnp.float32)
    teacher_logits, student_logits = (
        lax.psum_scatter(teacher_partial, "dp", scatter_dimension=0, tiled=True),
        lax.psum_scatter(student_partial, "dp", scatter_dimension=0, tiled=True),
    )
    first_row = lax.axis_index("dp") * share
    chosen = lax.dynamic_slice_in_dim(actions, first_row, share)
    benefit = lax.dynamic_slice_in_dim(advantages, first_row, share)
    weight = lax.dynamic_slice_in_dim(loss_mask, first_row, share).astype(jnp.float32)
    vocab_shard = teacher_logits.shape[1]
    columns = lax.axis_index("fsdp") * vocab_shard + jnp.arange(vocab_shard, dtype=jnp.int32)
    onehot = (chosen[:, None] == columns[None, :]).astype(jnp.float32)
    local_pick = jnp.sum(onehot * student_logits, axis=1)
    teacher_max, student_max = lax.pmax(
        (jnp.max(teacher_logits, axis=1), jnp.max(student_logits, axis=1)), "fsdp"
    )
    teacher_exp = jnp.exp(teacher_logits - teacher_max[:, None])
    student_exp = jnp.exp(student_logits - student_max[:, None])
    teacher_sum, student_sum, cross, pick = lax.psum(
        (
            jnp.sum(teacher_exp, axis=1),
            jnp.sum(student_exp, axis=1),
            jnp.sum(teacher_exp * (teacher_logits - student_logits), axis=1),
            local_pick,
        ),
        "fsdp",
    )
    teacher_lse = teacher_max + jnp.log(teacher_sum)
    student_lse = student_max + jnp.log(student_sum)
    kl = cross / teacher_sum - teacher_lse + student_lse
    action_logp = pick - student_lse
    losses = weight * (kl_weight * kl - benefit * action_logp)
    teacher_prob = teacher_exp / teacher_sum[:, None]
    student_prob = student_exp / student_sum[:, None]
    logit_grad = (
        weight[:, None]
        * (kl_weight * (student_prob - teacher_prob) + benefit[:, None] * (student_prob - onehot))
    ).astype(jnp.bfloat16)
    grad_all = lax.all_gather(logit_grad, "dp", axis=0, tiled=True)
    head_grad = lax.dot_general(
        student_rows, grad_all, (((0,), (0,)), ((), ())), preferred_element_type=jnp.float32
    )
    hidden_grad = lax.psum_scatter(
        lax.dot_general(
            grad_all, student_head, (((1,), (1,)), ((), ())), preferred_element_type=jnp.float32
        ),
        "fsdp",
        scatter_dimension=0,
        tiled=True,
    ).astype(jnp.bfloat16)
    return (losses, head_grad, hidden_grad)


def solution(mesh):
    placed = (
        P(("fsdp", "dp"), None),
        P(("fsdp", "dp"), None),
        P("dp", "fsdp"),
        P("dp", "fsdp"),
        P(),
        P(),
        P(),
    )
    return jax.shard_map(
        shards,
        mesh=mesh,
        in_specs=placed,
        out_specs=(P("dp"), P("dp", "fsdp"), P("fsdp", "dp")),
        check_vma=False,
    )
```

profile of v0, /device:TPU:0, one launch (start us, length us, event | category | flops | bytes accessed | tf_op | source)
XLA Modules:
  0.0 882.2 jit_solution(9315248481486084040)
XLA Ops:
  7.2 0.0 all-gather.6.cloned.1.call-start
  7.2 11.0 %all_to_all.38 = bf16[8,4,1024]{2,0,1:T(8,128)(2,1)} all-to-all(bf16[8,4,1024]{2,0,1:T(8,128)(2,1)} %bitcast.21), channel_id=1, replica_groups=mesh['fsdp'=32,'dp'=4] {'dp'}, dimensions={1} | all-to-all | bytes 131072 | tf_op jit(solution)/shard_map/all_to_all | solution.py:14
  18.2 0.0 all-gather.6.cloned.1.call-update
  18.2 0.0 all-gather.4.cloned.1.call-start
  18.3 10.1 %all_to_all.39 = bf16[8,4,2048]{2,0,1:T(8,128)(2,1)} all-to-all(bf16[8,4,2048]{2,0,1:T(8,128)(2,1)} %bitcast.20), channel_id=1, replica_groups=mesh['fsdp'=32,'dp'=4] {'dp'}, dimensions={1} | all-to-all | bytes 262144 | tf_op jit(solution)/shard_map/all_to_all | solution.py:13
  28.4 0.0 all-gather.4.cloned.1.call-update
  28.4 0.0 reduce-scatter.6.cloned.1.call-start
  28.5 141.8 %all-gather.6.cloned.1.call-done = bf16[1024,1024]{1,0:T(8,128)(2,1)} async-done(((bf16[32,1024]{1,0:T(8,128)(2,1)}), bf16[1024,1024]{1,0:T(8,128)(2,1)}) %all-gather.6.cloned.1.call-update) | async-done | bytes 2097168 | tf_op jit(solution)/shard_map/all_gather | solution.py:18
  170.3 10.5 %fusion.9 = f32[1024,2048]{1,0:T(8,128)} fusion(bf16[1024,1024]{1,0:T(8,128)(2,1)} %all-gather.6.cloned.1.call-done, bf16[1024,2048]{1,0:T(8,128)(2,1)} %param.10), kind=kOutput, calls=%fused_computation.18 | convolution fusion | flops 4294967296 | bytes 14680064 | tf_op jit(solution)/shard_map/dot_general | solution.py:23
  180.8 0.0 reduce-scatter.6.cloned.1.call-update
  180.8 0.0 reduce-scatter.4.cloned.1.call-start
  180.9 147.8 %all-gather.4.cloned.1.call-done = bf16[1024,2048]{1,0:T(8,128)(2,1)} async-done(((bf16[32,2048]{1,0:T(8,128)(2,1)}), bf16[1024,2048]{1,0:T(8,128)(2,1)}) %all-gather.4.cloned.1.call-update) | async-done | bytes 4194320 | tf_op jit(solution)/shard_map/all_gather | solution.py:17
  328.7 14.8 %fusion.8 = f32[1024,2048]{1,0:T(8,128)} fusion(bf16[1024,2048]{1,0:T(8,128)(2,1)} %all-gather.4.cloned.1.call-done, bf16[2048,2048]{1,0:T(8,128)(2,1)} %param.9), kind=kOutput, calls=%fused_computation.17 | convolution fusion | flops 8589934592 | bytes 20971520 | tf_op jit(solution)/shard_map/dot_general | solution.py:22
  343.4 0.0 reduce-scatter.4.cloned.1.call-update
  343.4 0.0 all-gather.8.cloned.1.call-start
  343.5 0.8 dynamic_slice.11
  344.3 66.0 %reduce-scatter.6.cloned.1.call-done = f32[256,2048]{1,0:T(8,128)} async-done(((f32[1024,2048]{1,0:T(8,128)}), f32[256,2048]{1,0:T(8,128)}) %reduce-scatter.6.cloned.1.call-update) | async-done | bytes 2097168 | tf_op jit(solution)/shard_map/reduce_scatter | solution.py:26
  410.3 0.0 copy-start
  410.3 1.9 reduce_max.19
  412.2 78.9 %reduce-scatter.4.cloned.1.call-done = f32[256,2048]{1,0:T(8,128)} async-done(((f32[1024,2048]{1,0:T(8,128)}), f32[256,2048]{1,0:T(8,128)}) %reduce-scatter.4.cloned.1.call-update) | async-done | bytes 2097168 | tf_op jit(solution)/shard_map/reduce_scatter | solution.py:25
  491.1 1.8 reduce_max.18
  492.9 81.8 %all-reduce.1 = (f32[256]{0:T(256)S(1)}, f32[256]{0:T(256)S(1)}) all-reduce(f32[256]{0:T(256)S(1)} %reduce_max.18, f32[256]{0:T(256)S(1)} %reduce_max.19), channel_id=1, replica_groups=mesh['fsdp'=32,'dp'=4] {'fsdp'}, use_global_device_ids=true, to_apply=%region_2.0 | all-reduce | flops 512 | bytes 4096 | tf_op jit(solution)/shard_map/pmax | solution.py:36
  574.6 0.0 copy-done
  574.7 2.8 multiply_reduce_fusion
  577.5 76.8 %all-reduce = (f32[256]{0:T(256)S(1)}, f32[256]{0:T(256)S(1)}, f32[256]{0:T(256)S(1)}, f32[256]{0:T(256)S(1)}) all-reduce(f32[256]{0:T(256)S(1)} %get-tuple-element.8, f32[256]{0:T(256)S(1)} %get-tuple-element.9, f32[256]{0:T(256)S(1)} %get-tuple-element.7, f32[256]{0:T(256)S(1)} %get-tuple-element.6), channel_id=1, replica_groups=mesh['fsdp'=32,'dp'=4] {'fsdp'}, use_global_device_ids=true, to_apply=%region_13.0 | all-reduce | flops 1024 | bytes 8192 | tf_op jit(solution)/shard_map/psum | solution.py:41
  654.3 1.3 subtract_multiply_fusion
  655.7 3.4 fusion.5
  659.1 0.0 all-gather.8.cloned.1.call-update
  659.1 0.2 reduce-scatter.8.cloned.1.call-start
  659.4 35.1 %all-gather.8.cloned.1.call-done = bf16[1024,2048]{1,0:T(8,128)(2,1)} async-done(((bf16[256,2048]{1,0:T(8,128)(2,1)}), bf16[1024,2048]{1,0:T(8,128)(2,1)}) %all-gather.8.cloned.1.call-update) | async-done | bytes 4194320 | tf_op jit(solution)/shard_map/all_gather | solution.py:61
  694.5 10.0 %fusion.10 = f32[1024,1024]{1,0:T(8,128)} fusion(bf16[1024,2048]{1,0:T(8,128)(2,1)} %all-gather.8.cloned.1.call-done, bf16[1024,2048]{1,0:T(8,128)(2,1)} %param.10), kind=kOutput, calls=%fused_computation.19 | convolution fusion | flops 4294967296 | bytes 12582912 | tf_op jit(solution)/shard_map/dot_general | solution.py:66
  704.5 0.0 copy-start.1
  704.5 0.0 reduce-scatter.8.cloned.1.call-update
  704.5 1.6 copy-done.1
  706.1 9.0 %convolution_bitcast_fusion = f32[1024,2048]{0,1:T(8,128)} fusion(bf16[1024,2048]{1,0:T(8,128)(2,1)} %all-gather.8.cloned.1.call-done, bf16[1024,1024]{1,0:T(8,128)(2,1)S(1)} %copy-done.1), kind=kOutput, calls=%fused_computation | convolution fusion | flops 4294967296 | bytes 14680064 | tf_op jit(solution)/shard_map/dot_general | solution.py:62
  715.1 9.1 %copy.10 = f32[1024,2048]{1,0:T(8,128)} copy(f32[1024,2048]{0,1:T(8,128)} %convolution_bitcast_fusion) | data formatting | bytes 16777216
  724.2 149.6 %reduce-scatter.8.cloned.1.call-done = f32[32,1024]{1,0:T(8,128)} async-done(((f32[1024,1024]{1,0:T(8,128)}), f32[32,1024]{1,0:T(8,128)}) %reduce-scatter.8.cloned.1.call-update) | async-done | bytes 131088 | tf_op jit(solution)/shard_map/reduce_scatter | solution.py:65
  873.8 1.5 convert_element_type.15
  (1 shorter events, 0.0 us)
Async XLA Ops:
  7.2 163.1 %all-gather.6.cloned.1.call-start = ((), (), s32[]{:S(2)}) async-start(), calls=%async_computation.7 | async-start | bytes 2162688 | tf_op jit(solution)/shard_map/all_gather | solution.py:18
  18.2 310.4 %all-gather.4.cloned.1.call-start = ((), (), s32[]{:S(2)}) async-start(), calls=%async_computation.5 | async-start | bytes 4325376 | tf_op jit(solution)/shard_map/all_gather | solution.py:17
  28.4 381.9 %reduce-scatter.6.cloned.1.call-start = ((), (), s32[]{:S(2)}) async-start(), calls=%async_computation.8 | async-start | bytes 10485760 | tf_op jit(solution)/shard_map/reduce_scatter | solution.py:26
  180.8 310.3 %reduce-scatter.4.cloned.1.call-start = ((), (), s32[]{:S(2)}) async-start(), calls=%async_computation.6 | async-start | bytes 10485760 | tf_op jit(solution)/shard_map/reduce_scatter | solution.py:25
  343.4 351.1 %all-gather.8.cloned.1.call-start = ((), (), s32[]{:S(2)}) async-start(), calls=%async_computation.9 | async-start | bytes 5242880 | tf_op jit(solution)/shard_map/all_gather | solution.py:61
  410.3 164.4 %copy-start = (f32[256,2048]{1,0:T(8,128)S(1)}, f32[256,2048]{1,0:T(8,128)}, u32[]{:S(2)}) copy-start(f32[256,2048]{1,0:T(8,128)} %reduce-scatter.6.cloned.1.call-done) | copy-start | bytes 6291460
  659.1 214.7 %reduce-scatter.8.cloned.1.call-start = ((), (), s32[]{:S(2)}) async-start(), calls=%async_computation.10 | async-start | bytes 4325376 | tf_op jit(solution)/shard_map/reduce_scatter | solution.py:65
  704.5 1.6 copy-start.1
Sparse Core Ops, SparseCore 0:
  18.4 151.8 all-gather.5
  171.9 156.6 all-gather.3
  331.3 78.8 reduce-scatter.5
  413.4 77.6 reduce-scatter.3
  659.3 35.1 all-gather.7
  704.6 169.1 reduce-scatter.7
where the time goes:
time: 883 us; the launch traced here: 882 us
  waiting for transfers between devices  619 us (70%)
  blocking collectives  180 us (20%)
  matrix products  44.3 us (5%)
  between operations  14.1 us (2%)
  other arithmetic  12.9 us (1%)
  local copies, waits for them, and re-layouts  11.5 us (1%)
    reduce_scatter x1, waiting for transfers between devices, shards(): lax.psum_scatter(lax.dot_general(grad_all, student_head, (((1,), (1,)), (...  150 us
    all_gather x1, waiting for transfers between devices, shards(): lax.all_gather(teacher_part, 'fsdp', axis=0, tiled=True)  148 us
    all_gather x1, waiting for transfers between devices, shards(): lax.all_gather(student_part, 'fsdp', axis=0, tiled=True)  142 us
    pmax x1, blocking collectives, shards(): lax.pmax((jnp.max(teacher_logits, axis=1), jnp.max(student_logits, axis=1...  81.8 us
    reduce_scatter x1, waiting for transfers between devices, shards(): lax.psum_scatter(teacher_partial, 'dp', scatter_dimension=0, tiled=True)  78.9 us
    psum x1, blocking collectives, shards(): lax.psum((jnp.sum(teacher_exp, axis=1), jnp.sum(student_exp, axis=1), jnp...  76.8 us
    reduce_scatter x1, waiting for transfers between devices, shards(): lax.psum_scatter(student_partial, 'dp', scatter_dimension=0, tiled=True)  66 us
    all_gather x1, waiting for transfers between devices, shards(): grad_all = lax.all_gather(logit_grad, 'dp', axis=0, tiled=True)  35.1 us
  transfers between devices with their start and end apart: 6, of which 6 were waited for; matrix products, arithmetic and copies ran while one was open for 5% of the time, Pallas kernels for 0%

commit v1 on v0

v1 whole, which is shorter than its diff:
```python
import jax
import jax.numpy as jnp
from jax import lax
from jax.sharding import PartitionSpec as P

kl_weight = 0.5
levels = 32767.0


def swap(x, bit):
    n = lax.axis_size("dp")
    return lax.ppermute(x, "dp", [(i, i ^ bit) for i in range(n)])


def spread(hidden):
    rows, width = hidden.shape
    quarters = lax.axis_size("dp")
    peers = lax.axis_size("fsdp")
    cut = hidden.reshape(rows, quarters, width // quarters).transpose(1, 0, 2)
    copies = jnp.broadcast_to(cut[:, None], (quarters, peers, rows, width // quarters))
    out = lax.all_to_all(
        copies.reshape(quarters * peers * rows, width // quarters),
        ("dp", "fsdp"),
        split_axis=0,
        concat_axis=0,
        tiled=True,
    )
    return out.reshape(quarters, peers * rows, width // quarters)


def block(x, index):
    return lax.dynamic_index_in_dim(x, index, 0, keepdims=False)


def product(x, head):
    return jnp.dot(x, head, preferred_element_type=jnp.float32)


def code(values):
    top = jnp.max(jnp.abs(values), axis=1, keepdims=True)
    ok = top > 1e-30
    step = jnp.where(ok, top / levels, 0.0)
    inverse = jnp.where(ok, levels / jnp.where(ok, top, 1.0), 0.0)
    return jnp.round(values * inverse).astype(jnp.int16), step


def partial_exchange(x, head, me):
    far_other = product(block(x, me ^ 3), head)
    far_got = swap(far_other, 1)
    far = product(block(x, me ^ 2), head) + far_got
    coded, step = code(far)
    coded_got, step_got = swap(coded, 2), swap(step, 2)
    near_other = product(block(x, me ^ 1), head)
    near_got = swap(near_other, 1)
    near = product(block(x, me), head) + near_got
    return near, coded_got, step_got, coded


def shards(
    teacher_hidden, student_hidden, teacher_head, student_head, actions, advantages, loss_mask
):
    me = lax.axis_index("dp")
    peers = lax.axis_size("fsdp")
    own_rows = teacher_hidden.shape[0]
    student_x = spread(student_hidden)
    student_near, student_coded, student_step, sent = partial_exchange(student_x, student_head, me)
    teacher_hidden, sent = lax.optimization_barrier((teacher_hidden, sent))
    teacher_x = spread(teacher_hidden)
    teacher_near, teacher_coded, teacher_step, _ = partial_exchange(teacher_x, teacher_head, me)
    student_logits = student_near + student_coded.astype(jnp.float32) * student_step
    teacher_logits = teacher_near + teacher_coded.astype(jnp.float32) * teacher_step

    def mine(a):
        return block(a.reshape(peers, -1, own_rows).transpose(1, 0, 2), me).reshape(-1)

    chosen, benefit = mine(actions), mine(advantages)
    weight = mine(loss_mask).astype(jnp.float32)
    vocab_shard = teacher_logits.shape[1]
    columns = lax.axis_index("fsdp") * vocab_shard + jnp.arange(vocab_shard, dtype=jnp.int32)
    onehot = (chosen[:, None] == columns[None, :]).astype(jnp.float32)
    teacher_top, student_top = jnp.max(teacher_logits, axis=1), jnp.max(student_logits, axis=1)
    teacher_exp = jnp.exp(teacher_logits - teacher_top[:, None])
    student_exp = jnp.exp(student_logits - student_top[:, None])
    stats = jnp.stack(
        [
            teacher_top,
            student_top,
            jnp.sum(teacher_exp, axis=1),
            jnp.sum(student_exp, axis=1),
            jnp.sum(teacher_exp * (teacher_logits - student_logits), axis=1),
            jnp.sum(onehot * student_logits, axis=1),
        ]
    )
    every = lax.all_to_all(
        jnp.broadcast_to(stats[None], (peers,) + stats.shape), "fsdp", 0, 0, tiled=True
    )
    teacher_max, student_max = jnp.max(every[:, 0], axis=0), jnp.max(every[:, 1], axis=0)
    teacher_part = jnp.exp(every[:, 0] - teacher_max)
    student_part = jnp.exp(every[:, 1] - student_max)
    teacher_sum = jnp.sum(every[:, 2] * teacher_part, axis=0)
    student_sum = jnp.sum(every[:, 3] * student_part, axis=0)
    cross = jnp.sum(every[:, 4] * teacher_part, axis=0)
    pick = jnp.sum(every[:, 5], axis=0)
    teacher_lse = teacher_max + jnp.log(teacher_sum)
    student_lse = student_max + jnp.log(student_sum)
    kl = cross / teacher_sum - teacher_lse + student_lse
    action_logp = pick - student_lse
    losses = weight * (kl_weight * kl - benefit * action_logp)
    teacher_prob = jnp.exp(teacher_logits - teacher_max[:, None]) * (1.0 / teacher_sum)[:, None]
    student_prob = jnp.exp(student_logits - student_max[:, None]) * (1.0 / student_sum)[:, None]
    grad = (
        weight[:, None]
        * (kl_weight * (student_prob - teacher_prob) + benefit[:, None] * (student_prob - onehot))
    ).astype(jnp.bfloat16)
    across = swap(grad, 2)
    beside = swap(grad, 1)
    grads = jnp.concatenate([grad, beside, across, swap(across, 1)], axis=0)
    student_rel = jnp.concatenate([block(student_x, me ^ i) for i in range(4)], axis=0)
    head_grad = lax.dot_general(
        student_rel, grads, (((0,), (0,)), ((), ())), preferred_element_type=jnp.float32
    )
    hidden_part = lax.dot_general(
        grads, student_head, (((1,), (1,)), ((), ())), preferred_element_type=jnp.float32
    ).astype(jnp.bfloat16)
    features = hidden_part.shape[1]
    hidden_part = hidden_part.reshape(4, peers, own_rows, features).transpose(1, 0, 2, 3)
    parts = lax.all_to_all(
        hidden_part.reshape(peers * 4 * own_rows, features), "fsdp", 0, 0, tiled=True
    )
    summed = jnp.sum(parts.reshape(peers, 4, own_rows, features).astype(jnp.float32), axis=0)

    def absolute(rel):
        return jnp.stack([block(rel, me ^ i) for i in range(4)])

    hidden_grad = absolute(summed).reshape(4 * own_rows, features).astype(jnp.bfloat16)
    pair = jnp.stack([losses, swap(losses, 1)])
    all_losses = absolute(jnp.concatenate([pair, swap(pair, 2)], axis=0))
    out_peers = peers // 4
    all_losses = lax.dynamic_slice_in_dim(
        all_losses.reshape(4, peers, own_rows), me * out_peers, out_peers, axis=1
    )
    token_loss = all_losses.transpose(1, 0, 2).reshape(-1)
    return (token_loss, head_grad, hidden_grad)


def solution(mesh):
    placed = (
        P(("fsdp", "dp"), None),
        P(("fsdp", "dp"), None),
        P("dp", "fsdp"),
        P("dp", "fsdp"),
        P(),
        P(),
        P(),
    )
    return jax.shard_map(
        shards,
        mesh=mesh,
        in_specs=placed,
        out_specs=(P("dp"), P("dp", "fsdp"), P("fsdp", "dp")),
        check_vma=False,
    )
```

time: 883 us -> 272 us (0.31)
  waiting for transfers between devices: 619 us -> 114 us
  blocking collectives: 180 us -> 56.8 us
  starting transfers between devices: 0.43 us -> 30.9 us
  between operations: 14.1 us -> 1.11 us
    all_gather x3 -> x0, waiting for transfers between devices: 325 us -> none  [the longest x1 148 us: shards(): lax.all_gather(teacher_part, 'fsdp', axis=0, tiled=True)]
    reduce_scatter x3 -> x0, waiting for transfers between devices: 294 us -> none  [the longest x1 150 us: shards(): lax.psum_scatter(lax.dot_general(grad_all, student_head, (((1,), (1,)), (...]
    pmax x1 -> x0, blocking collectives: 81.8 us -> none  [shards(): lax.pmax((jnp.max(teacher_logits, axis=1), jnp.max(student_logits, axis=1...]
    psum x1 -> x0, blocking collectives: 76.8 us -> none  [shards(): lax.psum((jnp.sum(teacher_exp, axis=1), jnp.sum(student_exp, axis=1), jnp...]
    ppermute x0 -> x13, waiting for transfers between devices: none -> 68.7 us  [swap(): return lax.ppermute(x, 'dp', [(i, i ^ bit) for i in range(n)])]
    all_to_all x0 -> x3, waiting for transfers between devices: none -> 45 us  [the longest x1 29.8 us: spread(): lax.all_to_all(copies.reshape(quarters * peers * rows, width // quarters)...]
    all_to_all x2 -> x1, blocking collectives: 21.1 us -> 56.8 us  [spread(): lax.all_to_all(copies.reshape(quarters * peers * rows, width // quarters)...]
    all_to_all x0 -> x3, starting transfers between devices: none -> 19.6 us  [the longest x1 11.2 us: spread(): lax.all_to_all(copies.reshape(quarters * peers * rows, width // quarters)...]
  transfers between devices with their start and end apart: 6 -> 16, of which waited for: 6 -> 9; matrix products, arithmetic and copies ran while one was open for 5% -> 11% of each run, Pallas kernels for 0% -> 0%
where the time goes in v1:
time: 272 us; the launch traced here: 268 us
  waiting for transfers between devices  114 us (42%)
  blocking collectives  56.8 us (21%)
  matrix products  43.3 us (16%)
  starting transfers between devices  30.9 us (11%)
  local copies, waits for them, and re-layouts  13 us (5%)
  other arithmetic  9.11 us (3%)
    ppermute x13, waiting for transfers between devices, swap(): return lax.ppermute(x, 'dp', [(i, i ^ bit) for i in range(n)])  68.7 us
    all_to_all x1, blocking collectives, spread(): lax.all_to_all(copies.reshape(quarters * peers * rows, width // quarters)...  56.8 us
    all_to_all x1, waiting for transfers between devices, spread(): lax.all_to_all(copies.reshape(quarters * peers * rows, width // quarters)...  29.8 us
    dot_general x8, matrix products, product(): return jnp.dot(x, head, preferred_element_type=jnp.float32)  25.3 us
    ppermute x13, starting transfers between devices, swap(): return lax.ppermute(x, 'dp', [(i, i ^ bit) for i in range(n)])  11.3 us
    all_to_all x1, starting transfers between devices, spread(): lax.all_to_all(copies.reshape(quarters * peers * rows, width // quarters)...  11.2 us
    dot_general x1, matrix products, shards(): lax.dot_general(student_rel, grads, (((0,), (0,)), ((), ())), preferred_e...  10.5 us
    all_to_all x1, waiting for transfers between devices, shards(): lax.all_to_all(hidden_part.reshape(peers * 4 * own_rows, features), 'fsdp...  10.4 us
  transfers between devices with their start and end apart: 16, of which 9 were waited for; matrix products, arithmetic and copies ran while one was open for 11% of the time, Pallas kernels for 0%

profile of v1, /device:TPU:0, one launch (start us, length us, event | category | flops | bytes accessed | tf_op | source)
XLA Modules:
  0.0 267.8 jit_solution(4198869151873811206)
XLA Ops:
  0.6 2.4 broadcast_in_dim.17
  3.0 11.2 %all-to-all-start = ((bf16[128,8,1024]{2,1,0:T(8,128)(2,1)}), bf16[128,8,1024]{2,1,0:T(8,128)(2,1)S(1)}, u32[]{:S(2)}, u32[]{:S(2)}) async-start(bf16[128,8,1024]{2,1,0:T(8,128)(2,1)} %bitcast.108), calls=%async_computation | async-start | bytes 4194304 | tf_op jit(solution)/shard_map/all_to_all | solution.py:21
  14.2 29.8 %all-to-all-done = bf16[128,8,1024]{2,1,0:T(8,128)(2,1)S(1)} async-done(((bf16[128,8,1024]{2,1,0:T(8,128)(2,1)}), bf16[128,8,1024]{2,1,0:T(8,128)(2,1)S(1)}, u32[]{:S(2)}, u32[]{:S(2)}) %all-to-all-start) | async-done | bytes 2097184 | tf_op jit(solution)/shard_map/all_to_all | solution.py:21
  44.0 0.2 dynamic-slice_bitcast_fusion.1
  44.2 2.4 copy-done.1
  46.6 1.2 fusion.49
  47.8 0.1 collective-permute-start
  47.9 4.1 %collective-permute-done = f32[256,2048]{1,0:T(8,128)S(1)} collective-permute-done((f32[256,2048]{1,0:T(8,128)S(1)}, f32[256,2048]{1,0:T(8,128)S(1)}, u32[]{:S(2)}, u32[]{:S(2)}) %collective-permute-start) | collective-permute-done | bytes 2097184 | tf_op jit(solution)/shard_map/ppermute | solution.py:12
  52.1 1.4 abs_reduce_fusion.1
  53.5 0.0 slice-start
  53.5 0.4 round-nearest-even_convert_fusion.1
  53.9 0.5 copy-done.7
  54.4 0.5 broadcast_in_dim.20
  54.9 0.0 slice-start.1
  54.9 56.8 %all_to_all.32 = bf16[128,8,2048]{2,1,0:T(8,128)(2,1)S(1)} all-to-all(bf16[128,8,2048]{2,1,0:T(8,128)(2,1)S(1)} %bitcast.105), channel_id=1, replica_groups=mesh['fsdp'=32,'dp'=4] {'dp','fsdp'}, dimensions={0} | all-to-all | bytes 8388608 | tf_op jit(solution)/shard_map/all_to_all | solution.py:21
  111.8 2.3 fusion.17
  114.1 0.1 collective-permute-start.2
  114.2 2.6 fusion.50
  116.8 0.5 collective-permute-start.5
  117.3 1.0 collective-permute-start.6
  118.3 3.6 %fusion.20 = f32[256,2048]{1,0:T(8,128)} fusion(bf16[2048,2048]{1,0:T(8,128)(2,1)S(1)} %bitcast.132, bf16[4,256,2048]{2,1,0:T(8,128)(2,1)S(1)} %bitcast.110, s32[]{:T(128)S(6)} %select_n.106), kind=kOutput, calls=%fused_computation.37 | convolution fusion | flops 2147483648 | bytes 11534340 | tf_op jit(solution)/shard_map/dot_general | solution.py:36
  121.9 2.5 abs_reduce_fusion
  124.4 1.3 round-nearest-even_convert_fusion
  125.7 2.5 collective-permute-start.3
  128.3 0.1 reshape.253
  128.4 1.1 collective-permute-start.7
  129.5 0.1 dynamic-slice_reduce_fusion
  129.6 0.1 eq.15
  129.7 2.6 collective-permute-start.4
  132.3 34.2 %collective-permute-done.7 = f32[256,1]{0,1:T(1,128)S(1)} collective-permute-done((f32[256,1]{0,1:T(1,128)S(1)}, f32[256,1]{0,1:T(1,128)S(1)}, u32[]{:S(2)}, u32[]{:S(2)}) %collective-permute-start.7) | collective-permute-done | bytes 1056 | tf_op jit(solution)/shard_map/ppermute | solution.py:12
  166.5 1.0 copy-done.16
  167.5 4.6 %fusion.48 = (f32[256]{0:T(256)S(1)}, f32[256,2048]{1,0:T(8,128)S(1)}) fusion(f32[256]{0:T(256)S(1)} %bitcast.134, s16[256,2048]{1,0:T(8,128)(2,1)} %copy-done.16, f32[256,2048]{1,0:T(8,128)} %collective-permute-done.5, bf16[256,1024]{1,0:T(8,128)(2,1)S(1)} %get-tuple-element.21, bf16[1024,2048]{1,0:T(8,128)(2,1)} %param.10), kind=kOutput, calls=%fused_computation.102 | convolution fusion | flops 1076363008 | bytes 9963520 | tf_op jit(solution)/shard_map/dot_general | solution.py:36
  172.1 7.1 %fusion.47 = (f32[256]{0:T(256)S(1)}, f32[256,2048]{1,0:T(8,128)S(1)}) fusion(f32[256]{0:T(256)S(1)} %bitcast.133, s16[256,2048]{1,0:T(8,128)(2,1)} %collective-permute-done.3, f32[256,2048]{1,0:T(8,128)} %collective-permute-done.1, bf16[2048,2048]{1,0:T(8,128)(2,1)} %param.9, bf16[4,256,2048]{2,1,0:T(8,128)(2,1)} %bitcast.112, s32[]{:T(128)S(6)} %select_n.101), kind=kOutput, calls=%fused_computation.101 | convolution fusion | flops 2150104832 | bytes 14682116 | tf_op jit(solution)/shard_map/dot_general | solution.py:36
  179.2 1.2 multiply_reduce_fusion
  180.4 0.0 copy-done
  180.5 0.7 broadcast_in_dim.21
  181.2 4.0 %all-to-all-start.2 = ((f32[32,6,256]{2,1,0:T(8,128)}), f32[32,6,256]{2,1,0:T(8,128)S(1)}, u32[]{:S(2)}, u32[]{:S(2)}) async-start(f32[32,6,256]{2,1,0:T(8,128)} %broadcast_in_dim.21), calls=%async_computation.2 | async-start | bytes 524288 | tf_op jit(solution)/shard_map/all_to_all | solution.py:94
  185.2 0.1 reshape.254
  185.3 0.1 reshape.248
  185.5 0.5 broadcast.164
  186.0 1.9 fusion.43
  187.9 0.8 convert_element_type.55
  188.7 0.8 reshape.256
  189.5 4.8 %all-to-all-done.2 = f32[32,6,256]{2,1,0:T(8,128)S(1)} async-done(((f32[32,6,256]{2,1,0:T(8,128)}), f32[32,6,256]{2,1,0:T(8,128)S(1)}, u32[]{:S(2)}, u32[]{:S(2)}) %all-to-all-start.2) | async-done | bytes 196640 | tf_op jit(solution)/shard_map/all_to_all | solution.py:94
  194.3 0.2 fusion.46
  194.6 3.0 %fusion.7 = bf16[256,2048]{1,0:T(8,128)(2,1)S(1)} fusion(f32[256,2048]{1,0:T(8,128)} %copy-done, f32[256,2048]{1,0:T(8,128)S(1)} %get-tuple-element.54, f32[256]{0:T(256)S(1)} %reshape.256, f32[256]{0:T(256)S(1)} %get-tuple-element.42, f32[256]{0:T(256)S(1)} %get-tuple-element.30, f32[256]{0:T(256)S(1)} %get-tuple-element.41, f32[256]{0:T(256)S(1)} %get-tuple-element.29, ...), kind=kLoop, calls=%fused_computation.15 | loop fusion | flops 6815744 | bytes 5258240 | tf_op jit(solution)/shard_map/convert_element_type | solution.py:114
  197.6 1.7 collective-permute-start.11
  199.3 22.9 %collective-permute-done.11 = bf16[256,2048]{1,0:T(8,128)(2,1)S(1)} collective-permute-done((bf16[256,2048]{1,0:T(8,128)(2,1)S(1)}, bf16[256,2048]{1,0:T(8,128)(2,1)S(1)}, u32[]{:S(2)}, u32[]{:S(2)}) %collective-permute-start.11) | collective-permute-done | bytes 1048608 | tf_op jit(solution)/shard_map/ppermute | solution.py:12
  222.2 2.6 collective-permute-done.12
  224.8 7.5 %convolution_convert_fusion = bf16[1024,1024]{1,0:T(8,128)(2,1)S(1)} fusion(bf16[1024,2048]{1,0:T(8,128)(2,1)S(1)} %copy-done.2, bf16[256,2048]{1,0:T(8,128)(2,1)S(1)} %collective-permute-done.12, bf16[256,2048]{1,0:T(8,128)(2,1)S(1)} %collective-permute-done.11, bf16[256,2048]{1,0:T(8,128)(2,1)S(1)} %collective-permute-done.10, ...), kind=kOutput, calls=%fused_computation.33 | convolution fusion | flops 4312793088 | bytes 10485760 | tf_op jit(solution)/shard_map/dot_general | solution.py:122
  232.4 1.6 copy.60
  234.0 4.5 %all-to-all-start.3 = ((bf16[32,32,1024]{2,1,0:T(8,128)(2,1)}), bf16[32,32,1024]{2,1,0:T(8,128)(2,1)S(1)}, u32[]{:S(2)}, u32[]{:S(2)}) async-start(bf16[32,32,1024]{2,1,0:T(8,128)(2,1)} %bitcast.106), calls=%async_computation.3 | async-start | bytes 4194304 | tf_op jit(solution)/shard_map/all_to_all | solution.py:127
  238.4 0.1 convert_element_type.50
  238.5 0.1 reshape.255
  238.6 0.1 collective-permute-start.8
  238.7 1.1 collective-permute-done.8
  239.9 1.6 collective-permute-start.9
  241.4 3.7 %collective-permute-done.9 = f32[2,256]{1,0:T(2,128)S(1)} collective-permute-done((f32[2,256]{1,0:T(2,128)S(1)}, f32[2,256]{1,0:T(2,128)S(1)}, u32[]{:S(2)}, u32[]{:S(2)}) %collective-permute-start.9) | collective-permute-done | bytes 2080 | tf_op jit(solution)/shard_map/ppermute | solution.py:12
  245.2 0.1 reshape.257
  245.3 0.7 reshape.258
  245.9 10.5 %fusion.8 = f32[1024,2048]{1,0:T(8,128)} fusion(bf16[256,1024]{1,0:T(8,128)(2,1)} %copy-done.6, bf16[256,1024]{1,0:T(8,128)(2,1)S(1)} %get-tuple-element.24, bf16[256,1024]{1,0:T(8,128)(2,1)} %copy-done.5, bf16[256,1024]{1,0:T(8,128)(2,1)S(1)} %get-tuple-element.21, bf16[256,2048]{1,0:T(8,128)(2,1)} %copy-done.15, bf16[256,2048]{1,0:T(8,128)(2,1)} %copy-done.13, ...), kind=kOutput, calls=%fused_computation.16 | convolution fusion | flops 4320133120 | bytes 14680064 | tf_op jit(solution)/shard_map/dot_general | solution.py:119
  256.4 10.4 %all-to-all-done.3 = bf16[32,32,1024]{2,1,0:T(8,128)(2,1)S(1)} async-done(((bf16[32,32,1024]{2,1,0:T(8,128)(2,1)}), bf16[32,32,1024]{2,1,0:T(8,128)(2,1)S(1)}, u32[]{:S(2)}, u32[]{:S(2)}) %all-to-all-start.3) | async-done | bytes 2097184 | tf_op jit(solution)/shard_map/all_to_all | solution.py:127
  266.9 0.3 convert_reduce_fusion
  267.2 0.6 maximum_bitcast_fusion
  (57 shorter events, 0.3 us)
Async XLA Ops:
  3.0 41.0 %all-to-all-start = ((bf16[128,8,1024]{2,1,0:T(8,128)(2,1)}), bf16[128,8,1024]{2,1,0:T(8,128)(2,1)S(1)}, u32[]{:S(2)}, u32[]{:S(2)}) async-start(bf16[128,8,1024]{2,1,0:T(8,128)(2,1)} %bitcast.108), calls=%async_computation | async-start | bytes 4194304 | tf_op jit(solution)/shard_map/all_to_all | solution.py:21
  44.0 2.6 copy-start.1
  44.2 3.6 %copy-start.6 = (bf16[256,1024]{1,0:T(8,128)(2,1)}, bf16[256,1024]{1,0:T(8,128)(2,1)S(1)}, u32[]{:S(2)}) copy-start(bf16[256,1024]{1,0:T(8,128)(2,1)S(1)} %get-tuple-element.23) | copy-start | bytes 1572868
  44.2 70.0 %copy-start.5 = (bf16[256,1024]{1,0:T(8,128)(2,1)}, bf16[256,1024]{1,0:T(8,128)(2,1)S(1)}, u32[]{:S(2)}) copy-start(bf16[256,1024]{1,0:T(8,128)(2,1)S(1)} %get-tuple-element.22) | copy-start | bytes 1572868
  47.8 4.2 %collective-permute-start = (f32[256,2048]{1,0:T(8,128)S(1)}, f32[256,2048]{1,0:T(8,128)S(1)}, u32[]{:S(2)}, u32[]{:S(2)}) collective-permute-start(f32[256,2048]{1,0:T(8,128)S(1)} %fusion.49), channel_id=1, source_target_pairs={{0,1},{1,0},{2,3},{3,2},{4,5},{5,4},{6,7},{7,6},{8,9},{9,8},{10,11... | collective-permute-start | bytes 6291464 | tf_op jit(solution)/shard_map/ppermute | solution.py:12
  53.5 0.9 copy-start.7
  53.5 58.2 %slice-start = ((s8[8388608]{0:T(1024)(128)(4,1)}), s8[4194304]{0:T(1024)(128)(4,1)S(1)}, s32[]{:S(2)}) async-start(s8[8388608]{0:T(1024)(128)(4,1)} %bitcast.131), calls=%async_computation.4 | async-start | bytes 8388608
  54.9 56.8 %slice-start.1 = ((s8[8388608]{0:T(1024)(128)(4,1)}), s8[4194304]{0:T(1024)(128)(4,1)S(1)}, s32[]{:S(2)}) async-start(s8[8388608]{0:T(1024)(128)(4,1)} %bitcast.131), calls=%async_computation.5 | async-start | bytes 8388608
  111.7 10.2 %copy-start.3 = (bf16[128,8,2048]{2,1,0:T(8,128)(2,1)}, bf16[128,8,2048]{2,1,0:T(8,128)(2,1)S(1)}, u32[]{:S(2)}) copy-start(bf16[128,8,2048]{2,1,0:T(8,128)(2,1)S(1)} %all_to_all.32) | copy-start | bytes 12582916
  114.1 7.8 %collective-permute-start.2 = (f32[256,2048]{1,0:T(8,128)S(1)}, f32[256,2048]{1,0:T(8,128)S(1)}, u32[]{:S(2)}, u32[]{:S(2)}) collective-permute-start(f32[256,2048]{1,0:T(8,128)S(1)} %fusion.17), channel_id=1, source_target_pairs={{0,1},{1,0},{2,3},{3,2},{4,5},{5,4},{6,7},{7,6},{8,9},{9,8},{10,11... | collective-permute-start | bytes 6291464 | tf_op jit(solution)/shard_map/ppermute | solution.py:12
  116.8 12.9 %collective-permute-start.5 = (f32[256,2048]{1,0:T(8,128)}, f32[256,2048]{1,0:T(8,128)}, u32[]{:S(2)}, u32[]{:S(2)}) collective-permute-start(f32[256,2048]{1,0:T(8,128)} %fusion.50), channel_id=1, source_target_pairs={{0,1},{1,0},{2,3},{3,2},{4,5},{5,4},{6,7},{7,6},{8,9},{9,8},{10,11... | collective-permute-start | bytes 6291464 | tf_op jit(solution)/shard_map/ppermute | solution.py:12
  117.3 49.2 %collective-permute-start.6 = (s16[256,2048]{1,0:T(8,128)(2,1)S(1)}, s16[256,2048]{1,0:T(8,128)(2,1)S(1)}, u32[]{:S(2)}, u32[]{:S(2)}) collective-permute-start(s16[256,2048]{1,0:T(8,128)(2,1)S(1)} %round-nearest-even_convert_fusion.1), channel_id=1, source_target_pairs={{0,2},{1,3},{2,0},{3,1},{4,6},{5,7},{6,4},{7,5},{8,10},{9,11},{10,... | collective-permute-start | bytes 3145736 | tf_op jit(solution)/shard_map/ppermute | solution.py:12
  121.9 50.1 %collective-permute-start.1 = (f32[256,2048]{1,0:T(8,128)}, f32[256,2048]{1,0:T(8,128)}, u32[]{:S(2)}, u32[]{:S(2)}) collective-permute-start(f32[256,2048]{1,0:T(8,128)} %fusion.20), channel_id=1, source_target_pairs={{0,1},{1,0},{2,3},{3,2},{4,5},{5,4},{6,7},{7,6},{8,9},{9,8},{10,11... | collective-permute-start | bytes 6291464 | tf_op jit(solution)/shard_map/ppermute | solution.py:12
  124.4 3.9 %copy-start.10 = (s32[1024]{0:T(1024)S(1)}, s32[1024]{0:T(1024)}, u32[]{:S(2)}) copy-start(s32[1024]{0:T(1024)} %param.11) | copy-start | bytes 12292
  125.7 46.3 %collective-permute-start.3 = (s16[256,2048]{1,0:T(8,128)(2,1)}, s16[256,2048]{1,0:T(8,128)(2,1)}, u32[]{:S(2)}, u32[]{:S(2)}) collective-permute-start(s16[256,2048]{1,0:T(8,128)(2,1)} %round-nearest-even_convert_fusion), channel_id=1, source_target_pairs={{0,2},{1,3},{2,0},{3,1},{4,6},{5,7},{6,4},{7,5},{8,10},{9,11},{10,... | collective-permute-start | bytes 3145736 | tf_op jit(solution)/shard_map/ppermute | solution.py:12
  128.4 38.0 %collective-permute-start.7 = (f32[256,1]{0,1:T(1,128)S(1)}, f32[256,1]{0,1:T(1,128)S(1)}, u32[]{:S(2)}, u32[]{:S(2)}) collective-permute-start(f32[256,1]{0,1:T(1,128)S(1)} %bitcast.129), channel_id=1, source_target_pairs={{0,2},{1,3},{2,0},{3,1},{4,6},{5,7},{6,4},{7,5},{8,10},{9,11},{10,... | collective-permute-start | bytes 3080 | tf_op jit(solution)/shard_map/ppermute | solution.py:12
  129.7 42.4 %collective-permute-start.4 = (f32[256,1]{0,1:T(1,128)S(1)}, f32[256,1]{0,1:T(1,128)S(1)}, u32[]{:S(2)}, u32[]{:S(2)}) collective-permute-start(f32[256,1]{0,1:T(1,128)S(1)} %bitcast.130), channel_id=1, source_target_pairs={{0,2},{1,3},{2,0},{3,1},{4,6},{5,7},{6,4},{7,5},{8,10},{9,11},{10,... | collective-permute-start | bytes 3080 | tf_op jit(solution)/shard_map/ppermute | solution.py:12
  166.5 1.0 copy-start.16
  179.1 1.3 copy-start
  179.1 6.1 %copy-start.11 = (f32[1024]{0:T(1024)S(1)}, f32[1024]{0:T(1024)}, u32[]{:S(2)}) copy-start(f32[1024]{0:T(1024)} %param.12) | copy-start | bytes 12292
  179.2 6.2 %copy-start.12 = (s32[1024]{0:T(1024)S(1)}, s32[1024]{0:T(1024)}, u32[]{:S(2)}) copy-start(s32[1024]{0:T(1024)} %param.13) | copy-start | bytes 12292
  181.2 13.1 %all-to-all-start.2 = ((f32[32,6,256]{2,1,0:T(8,128)}), f32[32,6,256]{2,1,0:T(8,128)S(1)}, u32[]{:S(2)}, u32[]{:S(2)}) async-start(f32[32,6,256]{2,1,0:T(8,128)} %broadcast_in_dim.21), calls=%async_computation.2 | async-start | bytes 524288 | tf_op jit(solution)/shard_map/all_to_all | solution.py:94
  194.6 30.3 %copy-start.2 = (bf16[1024,2048]{1,0:T(8,128)(2,1)S(1)}, bf16[1024,2048]{1,0:T(8,128)(2,1)}, u32[]{:S(2)}) copy-start(bf16[1024,2048]{1,0:T(8,128)(2,1)} %param.10) | copy-start | bytes 12582916
  197.6 34.8 %copy-start.4 = (bf16[256,2048]{1,0:T(8,128)(2,1)}, bf16[256,2048]{1,0:T(8,128)(2,1)S(1)}, u32[]{:S(2)}) copy-start(bf16[256,2048]{1,0:T(8,128)(2,1)S(1)} %fusion.7) | copy-start | bytes 3145732
  197.6 24.6 %collective-permute-start.11 = (bf16[256,2048]{1,0:T(8,128)(2,1)S(1)}, bf16[256,2048]{1,0:T(8,128)(2,1)S(1)}, u32[]{:S(2)}, u32[]{:S(2)}) collective-permute-start(bf16[256,2048]{1,0:T(8,128)(2,1)S(1)} %fusion.7), channel_id=1, source_target_pairs={{0,2},{1,3},{2,0},{3,1},{4,6},{5,7},{6,4},{7,5},{8,10},{9,11},{10,... | collective-permute-start | bytes 3145736 | tf_op jit(solution)/shard_map/ppermute | solution.py:12
  199.3 22.9 %collective-permute-start.10 = (bf16[256,2048]{1,0:T(8,128)(2,1)S(1)}, bf16[256,2048]{1,0:T(8,128)(2,1)S(1)}, u32[]{:S(2)}, u32[]{:S(2)}) collective-permute-start(bf16[256,2048]{1,0:T(8,128)(2,1)S(1)} %fusion.7), channel_id=1, source_target_pairs={{0,1},{1,0},{2,3},{3,2},{4,5},{5,4},{6,7},{7,6},{8,9},{9,8},{10,11... | collective-permute-start | bytes 3145736 | tf_op jit(solution)/shard_map/ppermute | solution.py:12
  222.2 10.2 %copy-start.13 = (bf16[256,2048]{1,0:T(8,128)(2,1)}, bf16[256,2048]{1,0:T(8,128)(2,1)S(1)}, u32[]{:S(2)}) copy-start(bf16[256,2048]{1,0:T(8,128)(2,1)S(1)} %collective-permute-done.11) | copy-start | bytes 3145732
  222.2 2.7 collective-permute-start.12
  222.2 10.2 %copy-start.14 = (bf16[256,2048]{1,0:T(8,128)(2,1)}, bf16[256,2048]{1,0:T(8,128)(2,1)S(1)}, u32[]{:S(2)}) copy-start(bf16[256,2048]{1,0:T(8,128)(2,1)S(1)} %collective-permute-done.10) | copy-start | bytes 3145732
  224.8 7.5 %copy-start.15 = (bf16[256,2048]{1,0:T(8,128)(2,1)}, bf16[256,2048]{1,0:T(8,128)(2,1)S(1)}, u32[]{:S(2)}) copy-start(bf16[256,2048]{1,0:T(8,128)(2,1)S(1)} %collective-permute-done.12) | copy-start | bytes 3145732
  234.0 4.5 %copy-start.9 = (f32[32,8]{1,0:T(8,128)S(1)}, f32[32,8]{1,0:T(8,128)}, u32[]{:S(2)}) copy-start(f32[32,8]{1,0:T(8,128)} %get-tuple-element.55) | copy-start | bytes 3076
  234.0 4.6 %copy-start.8 = (f32[32,8]{1,0:T(8,128)S(1)}, f32[32,8]{1,0:T(8,128)}, u32[]{:S(2)}) copy-start(f32[32,8]{1,0:T(8,128)} %get-tuple-element.14) | copy-start | bytes 3076
  234.0 32.9 %all-to-all-start.3 = ((bf16[32,32,1024]{2,1,0:T(8,128)(2,1)}), bf16[32,32,1024]{2,1,0:T(8,128)(2,1)S(1)}, u32[]{:S(2)}, u32[]{:S(2)}) async-start(bf16[32,32,1024]{2,1,0:T(8,128)(2,1)} %bitcast.106), calls=%async_computation.3 | async-start | bytes 4194304 | tf_op jit(solution)/shard_map/all_to_all | solution.py:127
  238.6 1.2 collective-permute-start.8
  239.9 5.2 %collective-permute-start.9 = (f32[2,256]{1,0:T(2,128)S(1)}, f32[2,256]{1,0:T(2,128)S(1)}, u32[]{:S(2)}, u32[]{:S(2)}) collective-permute-start(f32[2,256]{1,0:T(2,128)S(1)} %pad_maximum_fusion.5), channel_id=1, source_target_pairs={{0,2},{1,3},{2,0},{3,1},{4,6},{5,7},{6,4},{7,5},{8,10},{9,11},{10,... | collective-permute-start | bytes 6152 | tf_op jit(solution)/shard_map/ppermute | solution.py:12
